TPU v7x, 32 devices: a whole 2x2x4 slice. The times are simulated.
32 devices in a mesh: section: 2 (over x), row: 4 (over y, core), col: 4 (over z).
Axes of the slice: x: 2, y: 2, z: 4, core: 2. Of those that a mesh axis runs over, the one named last changes fastest.
Arguments:
- layer_input: bfloat16 [2, 2, 128, 8192], P('section', None, 'col', 'row'), may hold values from -6 to 6
- top_grad: bfloat16 [2, 128, 8192], P(None, 'col', 'row'), may hold values from -6 to 6
- gate_weight: bfloat16 [2, 8192, 14336], P('section', 'row', 'col'), may hold values from -0.0625 to 0.0625
- up_weight: bfloat16 [2, 8192, 14336], P('section', 'row', 'col'), may hold values from -0.0625 to 0.0625
- down_weight: bfloat16 [2, 14336, 8192], P('section', 'col', 'row'), may hold values from -0.046875 to 0.046875
- activity: int32 [2, 2, 2, 4, 28], P('section', None, None, 'col'), may hold values from 0 to 56, as said below
Outputs:
- sent_grad: bfloat16 [2, 2, 128, 8192], P('section', None, 'col', 'row')
- gate_grad: bfloat16 [2, 8192, 14336], P('section', 'row', 'col')
- up_grad: bfloat16 [2, 8192, 14336], P('section', 'row', 'col')
- down_grad: bfloat16 [2, 14336, 8192], P('section', 'col', 'row')
Inputs may be any that keep to these rules, and one draw needn't show every extreme that they name: `activity`: each list names distinct blocks below 56, then the value 56 marks empty slots up to the end; every list holds at least 7 blocks, and in every token block some column's list is full.
All inputs are finite; a program needn't handle non-finite values.
Results may differ from a plain program's by a relative error of at most 0.006.
Values may be sent and summed in bfloat16 or wider, within the bound.
No kernel may reach another device: no remote copies, remote signals or barrier semaphores. Data moves between devices by JAX's collectives and lax.ppermute only.
A program may use at most 384 MiB of HBM per device.

v0:
```python
import jax
import jax.numpy as jnp
from jax import lax
from jax.sharding import PartitionSpec as P

BLK = 64
TB = 64


def passed_along(value, axis, steps):
    count = lax.axis_size(axis)
    initial, last = (max(0, -steps), min(count, count - steps))
    return lax.ppermute(value, axis, [(source, source + steps) for source in range(initial, last)])


def activate(gate_total, up_total, grad_total, keep_mask):
    positive = jnp.maximum(gate_total, 0.0)
    squared = keep_mask * positive * positive
    hidden = (squared * up_total).astype(jnp.bfloat16)
    grad_up = (squared * grad_total).astype(jnp.bfloat16)
    grad_hgate = (keep_mask * 2.0 * positive * up_total * grad_total).astype(jnp.bfloat16)
    return (hidden, grad_hgate, grad_up)


def combine(gate_part, up_part, grad_part, keep_mask):
    gate_total, up_total, grad_total = (
        lax.psum_scatter(gate_part, "row", scatter_dimension=0, tiled=True),
        lax.psum_scatter(up_part, "row", scatter_dimension=0, tiled=True),
        lax.psum_scatter(grad_part, "row", scatter_dimension=0, tiled=True),
    )
    row_count = gate_total.shape[0]
    own_mask = lax.dynamic_slice_in_dim(keep_mask, lax.axis_index("row") * row_count, row_count, 0)
    results = activate(gate_total, up_total, grad_total, own_mask)
    hidden, grad_hgate, grad_up = (
        lax.all_gather(results[0], "row", axis=0, tiled=True),
        lax.all_gather(results[1], "row", axis=0, tiled=True),
        lax.all_gather(results[2], "row", axis=0, tiled=True),
    )
    return (hidden, grad_hgate, grad_up)


def shards(layer_input, top_grad, gate_weight, up_weight, down_weight, activity):
    sections = lax.axis_size("section")
    section_pos = lax.axis_index("section")
    inputs_all = layer_input[0]
    w_gate = gate_weight[0]
    w_up = up_weight[0]
    w_down = down_weight[0]
    lists_all = activity[0, :, :, 0, :]
    micro_count = inputs_all.shape[0]
    block_total = w_gate.shape[1] // BLK
    sum_gate = jnp.zeros(w_gate.shape, jnp.float32)
    sum_up = jnp.zeros(w_up.shape, jnp.float32)
    sum_down = jnp.zeros(w_down.shape, jnp.float32)
    sent = jnp.zeros(layer_input.shape, jnp.bfloat16)
    received = jnp.zeros(inputs_all.shape[1:], jnp.bfloat16)
    for tick_number in range(micro_count + sections - 1):
        micro_pos = tick_number - (sections - 1 - section_pos)
        usable = jnp.logical_and(micro_pos >= 0, micro_pos < micro_count)
        chosen = jnp.clip(micro_pos, 0, micro_count - 1)
        active_flag = usable.astype(jnp.float32)
        local_input = lax.dynamic_index_in_dim(inputs_all, chosen, 0, keepdims=False)
        top_local = lax.dynamic_index_in_dim(top_grad, chosen, 0, keepdims=False)
        grad_in = jnp.where(section_pos == sections - 1, top_local, received)
        rows_input, rows_grad = (
            lax.all_gather(local_input, "col", axis=0, tiled=True),
            lax.all_gather(grad_in, "col", axis=0, tiled=True),
        )
        block_list = lax.dynamic_index_in_dim(lists_all, chosen, 0, keepdims=False)
        tokens = rows_input.shape[0]
        block_count = tokens // TB
        blocks = jnp.arange(block_total, dtype=jnp.int32)
        block_on = (
            jnp.any(block_list[:, :, None] == blocks[None, None, :], axis=1).astype(jnp.float32)
            * active_flag
        )
        keep_mask = jnp.broadcast_to(
            block_on[:, None, :, None], (block_count, TB, block_total, BLK)
        ).reshape(tokens, block_total * BLK)
        gate_part = jnp.dot(rows_input, w_gate, preferred_element_type=jnp.float32)
        up_part = jnp.dot(rows_input, w_up, preferred_element_type=jnp.float32)
        grad_part = jnp.einsum("td,fd->tf", rows_grad, w_down, preferred_element_type=jnp.float32)
        hidden, grad_hgate, grad_up = combine(gate_part, up_part, grad_part, keep_mask)
        sum_gate = sum_gate + jnp.einsum(
            "td,tf->df", rows_input, grad_hgate, preferred_element_type=jnp.float32
        )
        sum_up = sum_up + jnp.einsum(
            "td,tf->df", rows_input, grad_up, preferred_element_type=jnp.float32
        )
        sum_down = sum_down + jnp.einsum(
            "tf,td->fd", hidden, rows_grad, preferred_element_type=jnp.float32
        )
        partial_back = jnp.einsum(
            "tf,df->td", grad_hgate, w_gate, preferred_element_type=jnp.float32
        )
        partial_back = partial_back + jnp.einsum(
            "tf,df->td", grad_up, w_up, preferred_element_type=jnp.float32
        )
        summed = lax.psum_scatter(partial_back, "col", scatter_dimension=0, tiled=True)
        handed = (grad_in.astype(jnp.float32) + summed).astype(jnp.bfloat16)
        written = lax.dynamic_update_slice(sent, handed[None, None], (0, chosen, 0, 0))
        sent = jnp.where(usable, written, sent)
        received = passed_along(handed, "section", -1)
    return (
        sent,
        sum_gate.astype(jnp.bfloat16)[None],
        sum_up.astype(jnp.bfloat16)[None],
        sum_down.astype(jnp.bfloat16)[None],
    )


def solution(mesh):
    in_specs = (
        P("section", None, "col", "row"),
        P(None, "col", "row"),
        P("section", "row", "col"),
        P("section", "row", "col"),
        P("section", "col", "row"),
        P("section", None, None, "col", None),
    )
    out_specs = (
        P("section", None, "col", "row"),
        P("section", "row", "col"),
        P("section", "row", "col"),
        P("section", "col", "row"),
    )
    return jax.shard_map(shards, mesh=mesh, in_specs=in_specs, out_specs=out_specs, check_vma=False)
```

profile of v0, /device:TPU:3, one launch (start us, length us, event | category | flops | bytes accessed | tf_op | source)
XLA Modules:
  0.0 651.4 jit_solution(17873560761817971865)
XLA Ops:
  8.9 14.5 %all-gather = bf16[1,1,128,2048]{3,2,1,0:T(8,128)(2,1)S(1)} all-gather(bf16[1,1,32,2048]{3,2,1,0:T(8,128)(2,1)S(1)} %get-tuple-element.18), channel_id=2, replica_groups=mesh['section'=2,'row'=4,'col'=4] {'col'}, dimensions={2}, use_global_device_ids=true | all-gather | bytes 655360 | tf_op jit(solution)/shard_map/all_gather | solution.py:66
  40.6 11.9 %all-gather.1 = bf16[1,128,2048]{2,1,0:T(8,128)(2,1)S(1)} all-gather(bf16[1,32,2048]{2,1,0:T(8,128)(2,1)S(1)} %dynamic-slice_select_fusion), channel_id=3, replica_groups=mesh['section'=2,'row'=4,'col'=4] {'col'}, dimensions={1}, use_global_device_ids=true | all-gather | bytes 655360 | tf_op jit(solution)/shard_map/all_gather | solution.py:67
  53.3 11.4 %fusion.4 = f32[128,3584]{1,0:T(8,128)} fusion(bf16[1,3584,2048]{2,1,0:T(8,128)(2,1)} %param.10, bf16[1,128,2048]{2,1,0:T(8,128)(2,1)S(1)} %all-gather.1), kind=kOutput, calls=%fused_computation.7 | convolution fusion | flops 1879048192 | bytes 17039360 | tf_op jit(solution)/shard_map/td,fd->tf/dot_general | solution.py:82
  70.1 27.3 %reduce-scatter.13.cloned.1.call-done = f32[32,3584]{1,0:T(8,128)} async-done(((f32[128,3584]{1,0:T(8,128)}), f32[32,3584]{1,0:T(8,128)}) %reduce-scatter.13.cloned.1.call-update) | async-done | bytes 458768 | tf_op jit(solution)/shard_map/reduce_scatter | solution.py:27
  97.4 32.2 %reduce-scatter.17.cloned.1.call-done = f32[32,3584]{1,0:T(8,128)} async-done(((f32[128,3584]{1,0:T(8,128)}), f32[32,3584]{1,0:T(8,128)}) %reduce-scatter.17.cloned.1.call-update) | async-done | bytes 458768 | tf_op jit(solution)/shard_map/reduce_scatter | solution.py:29
  171.6 17.7 %all-gather.2 = bf16[1,1,128,2048]{3,2,1,0:T(8,128)(2,1)S(1)} all-gather(bf16[1,1,32,2048]{3,2,1,0:T(8,128)(2,1)S(1)} %get-tuple-element.19), channel_id=4, replica_groups=mesh['section'=2,'row'=4,'col'=4] {'col'}, dimensions={2}, use_global_device_ids=true | all-gather | bytes 655360 | tf_op jit(solution)/shard_map/all_gather | solution.py:66
  212.0 13.8 %all_gather.50 = bf16[128,2048]{1,0:T(8,128)(2,1)S(1)} all-gather(bf16[32,2048]{1,0:T(8,128)(2,1)S(1)} %bitcast_select_fusion.2), channel_id=1, replica_groups=mesh['section'=2,'row'=4,'col'=4] {'col'}, dimensions={0}, use_global_device_ids=true | all-gather | bytes 655360 | tf_op jit(solution)/shard_map/all_gather | solution.py:67
  225.8 11.6 %fusion.2 = f32[128,3584]{1,0:T(8,128)} fusion(bf16[128,2048]{1,0:T(8,128)(2,1)S(1)} %all_gather.50, bf16[1,3584,2048]{2,1,0:T(8,128)(2,1)} %param.10), kind=kOutput, calls=%fused_computation.5 | convolution fusion | flops 1879048192 | bytes 17039360 | tf_op jit(solution)/shard_map/td,fd->tf/dot_general | solution.py:82
  243.7 24.6 %reduce-scatter.21.cloned.1.call-done = f32[32,3584]{1,0:T(8,128)} async-done(((f32[128,3584]{1,0:T(8,128)}), f32[32,3584]{1,0:T(8,128)}) %reduce-scatter.21.cloned.1.call-update) | async-done | bytes 458768 | tf_op jit(solution)/shard_map/reduce_scatter | solution.py:27
  268.3 32.1 %reduce-scatter.25.cloned.1.call-done = f32[32,3584]{1,0:T(8,128)} async-done(((f32[128,3584]{1,0:T(8,128)}), f32[32,3584]{1,0:T(8,128)}) %reduce-scatter.25.cloned.1.call-update) | async-done | bytes 458768 | tf_op jit(solution)/shard_map/reduce_scatter | solution.py:29
  344.9 18.2 %all-gather.3 = bf16[1,1,128,2048]{3,2,1,0:T(8,128)(2,1)S(1)} all-gather(bf16[1,1,32,2048]{3,2,1,0:T(8,128)(2,1)} %get-tuple-element.17), channel_id=5, replica_groups=mesh['section'=2,'row'=4,'col'=4] {'col'}, dimensions={2}, use_global_device_ids=true | all-gather | bytes 655360 | tf_op jit(solution)/shard_map/all_gather | solution.py:66
  386.6 12.6 %all_gather.57 = bf16[128,3584]{1,0:T(8,128)(2,1)S(1)} all-gather(bf16[32,3584]{1,0:T(8,128)(2,1)} %get-tuple-element.11), channel_id=1, replica_groups=mesh['section'=2,'row'=4,'col'=4] {'row'}, dimensions={0}, use_global_device_ids=true | all-gather | bytes 1146880 | tf_op jit(solution)/shard_map/all_gather | solution.py:35
  399.3 12.7 %fusion.52 = f32[3584,2048]{1,0:T(8,128)} fusion(bf16[128,3584]{1,0:T(8,128)(2,1)S(1)} %all_gather.57, bf16[1,128,2048]{2,1,0:T(8,128)(2,1)} %copy-done.4), kind=kOutput, calls=%fused_computation.52 | convolution fusion | flops 1879048192 | bytes 30801920 | tf_op jit(solution)/shard_map/tf,td->fd/dot_general | solution.py:90
  412.0 12.3 %fusion.57 = f32[2048,3584]{1,0:T(8,128)} fusion(bf16[128,3584]{1,0:T(8,128)(2,1)S(1)} %all_gather.47, bf16[1,1,128,2048]{3,2,1,0:T(8,128)(2,1)S(1)} %all-gather), kind=kOutput, calls=%fused_computation.57 | convolution fusion | flops 1879048192 | bytes 30801920 | tf_op jit(solution)/shard_map/td,tf->df/dot_general | solution.py:84
  428.4 12.0 %fusion.55 = f32[2048,3584]{1,0:T(8,128)} fusion(bf16[128,3584]{1,0:T(8,128)(2,1)S(1)} %all_gather.48, bf16[1,1,128,2048]{3,2,1,0:T(8,128)(2,1)S(1)} %all-gather), kind=kOutput, calls=%fused_computation.55 | convolution fusion | flops 1879048192 | bytes 30801920 | tf_op jit(solution)/shard_map/td,tf->df/dot_general | solution.py:87
  440.4 13.6 %all_gather.54 = bf16[128,2048]{1,0:T(8,128)(2,1)S(1)} all-gather(bf16[32,2048]{1,0:T(8,128)(2,1)S(1)} %bitcast_select_fusion), channel_id=1, replica_groups=mesh['section'=2,'row'=4,'col'=4] {'col'}, dimensions={0}, use_global_device_ids=true | all-gather | bytes 655360 | tf_op jit(solution)/shard_map/all_gather | solution.py:67
  454.0 11.5 %fusion = f32[128,3584]{1,0:T(8,128)} fusion(bf16[128,2048]{1,0:T(8,128)(2,1)S(1)} %all_gather.54, bf16[1,3584,2048]{2,1,0:T(8,128)(2,1)} %param.10), kind=kOutput, calls=%fused_computation.3 | convolution fusion | flops 1879048192 | bytes 17039360 | tf_op jit(solution)/shard_map/td,fd->tf/dot_general | solution.py:82
  465.8 12.4 %fusion.48 = f32[2048,3584]{1,0:T(8,128)} fusion(bf16[128,3584]{1,0:T(8,128)(2,1)S(1)} %copy-done.3, bf16[1,1,128,2048]{3,2,1,0:T(8,128)(2,1)S(1)} %all-gather.2), kind=kOutput, calls=%fused_computation.48 | convolution fusion | flops 1879048192 | bytes 30801920 | tf_op jit(solution)/shard_map/td,tf->df/dot_general | solution.py:84
  478.1 14.8 %all_gather.58 = bf16[128,3584]{1,0:T(8,128)(2,1)S(1)} all-gather(bf16[32,3584]{1,0:T(8,128)(2,1)S(1)} %copy-done.15), channel_id=1, replica_groups=mesh['section'=2,'row'=4,'col'=4] {'row'}, dimensions={0}, use_global_device_ids=true | all-gather | bytes 1146880 | tf_op jit(solution)/shard_map/all_gather | solution.py:35
  492.9 11.9 %fusion.46 = f32[2048,3584]{1,0:T(8,128)} fusion(bf16[128,3584]{1,0:T(8,128)(2,1)S(1)} %copy-done.1, bf16[1,1,128,2048]{3,2,1,0:T(8,128)(2,1)S(1)} %all-gather.2), kind=kOutput, calls=%fused_computation.46 | convolution fusion | flops 1879048192 | bytes 30801920 | tf_op jit(solution)/shard_map/td,tf->df/dot_general | solution.py:87
  504.8 11.6 %fusion.70 = f32[3584,2048]{1,0:T(8,128)} fusion(bf16[128,3584]{1,0:T(8,128)(2,1)S(1)} %all_gather.58, bf16[128,2048]{1,0:T(8,128)(2,1)S(1)} %copy-done.6), kind=kOutput, calls=%fused_computation.98 | convolution fusion | flops 1879048192 | bytes 30801920 | tf_op jit(solution)/shard_map/tf,td->fd/dot_general | solution.py:90
  567.3 25.2 %fusion.30 = bf16[1,2048,3584]{2,1,0:T(8,128)(2,1)} fusion(bf16[128,3584]{1,0:T(8,128)(2,1)S(1)} %all_gather.55, f32[2048,3584]{1,0:T(8,128)} %fusion.57, f32[2048,3584]{1,0:T(8,128)} %fusion.48, bf16[1,1,128,2048]{3,2,1,0:T(8,128)(2,1)S(1)} %all-gather.3), kind=kOutput, calls=%fused_computation.33 | convolution fusion | flops 1901068288 | bytes 74842112 | tf_op jit(solution)/shard_map/td,tf->df/dot_general | solution.py:84
  592.5 24.9 %fusion.32 = bf16[1,3584,2048]{2,1,0:T(8,128)(2,1)} fusion(bf16[128,3584]{1,0:T(8,128)(2,1)S(1)} %all_gather.59, bf16[128,2048]{1,0:T(8,128)(2,1)S(1)} %copy-done.8, f32[3584,2048]{1,0:T(8,128)} %fusion.52, f32[3584,2048]{1,0:T(8,128)} %fusion.70), kind=kOutput, calls=%fused_computation.35 | convolution fusion | flops 1901068288 | bytes 74842112 | tf_op jit(solution)/shard_map/tf,td->fd/dot_general | solution.py:90
  617.4 25.0 %fusion.31 = bf16[1,2048,3584]{2,1,0:T(8,128)(2,1)} fusion(bf16[128,3584]{1,0:T(8,128)(2,1)S(1)} %all_gather.56, f32[2048,3584]{1,0:T(8,128)} %fusion.55, f32[2048,3584]{1,0:T(8,128)} %fusion.46, bf16[1,1,128,2048]{3,2,1,0:T(8,128)(2,1)S(1)} %all-gather.3), kind=kOutput, calls=%fused_computation.34 | convolution fusion | flops 1901068288 | bytes 74842112 | tf_op jit(solution)/shard_map/td,tf->df/dot_general | solution.py:87
  (113 shorter events, 220.7 us)
Async XLA Ops:
  7.2 62.9 %reduce-scatter.15.cloned.1.call-start = ((), (), s32[]{:S(2)}) async-start(), calls=%async_computation.13 | async-start | bytes 2293760 | tf_op jit(solution)/shard_map/reduce_scatter | solution.py:28
  31.9 65.4 %reduce-scatter.13.cloned.1.call-start = ((), (), s32[]{:S(2)}) async-start(), calls=%async_computation.12 | async-start | bytes 2293760 | tf_op jit(solution)/shard_map/reduce_scatter | solution.py:27
  40.5 24.3 %copy-start.16 = (s32[1,2,2,1,28]{4,3,2,1,0:T(1,128)S(1)}, s32[1,2,2,1,28]{4,3,2,1,0:T(1,128)}, u32[]{:S(2)}) copy-start(s32[1,2,2,1,28]{4,3,2,1,0:T(1,128)} %param.11) | copy-start | bytes 1348
  40.5 89.1 %reduce-scatter.17.cloned.1.call-start = ((), (), s32[]{:S(2)}) async-start(), calls=%async_computation.14 | async-start | bytes 2293760 | tf_op jit(solution)/shard_map/reduce_scatter | solution.py:29
  64.7 141.9 %reduce-scatter.19.cloned.1.call-start = ((), (), s32[]{:S(2)}) async-start(), calls=%async_computation.15 | async-start | bytes 1310720 | tf_op jit(solution)/shard_map/reduce_scatter | solution.py:99
  171.6 72.1 %reduce-scatter.23.cloned.1.call-start = ((), (), s32[]{:S(2)}) async-start(), calls=%async_computation.17 | async-start | bytes 2293760 | tf_op jit(solution)/shard_map/reduce_scatter | solution.py:28
  197.9 70.4 %reduce-scatter.21.cloned.1.call-start = ((), (), s32[]{:S(2)}) async-start(), calls=%async_computation.16 | async-start | bytes 2293760 | tf_op jit(solution)/shard_map/reduce_scatter | solution.py:27
  206.6 93.9 %reduce-scatter.25.cloned.1.call-start = ((), (), s32[]{:S(2)}) async-start(), calls=%async_computation.18 | async-start | bytes 2293760 | tf_op jit(solution)/shard_map/reduce_scatter | solution.py:29
  207.7 4.3 collective-permute-start
  225.8 76.9 %copy-start.5 = (bf16[128,2048]{1,0:T(8,128)(2,1)}, bf16[128,2048]{1,0:T(8,128)(2,1)S(1)}, u32[]{:S(2)}) copy-start(bf16[128,2048]{1,0:T(8,128)(2,1)S(1)} %all_gather.50) | copy-start | bytes 1572868
  237.4 186.9 %reduce-scatter.27.cloned.1.call-start = ((), (), s32[]{:S(2)}) async-start(), calls=%async_computation.19 | async-start | bytes 1310720 | tf_op jit(solution)/shard_map/reduce_scatter | solution.py:99
  344.8 171.6 %reduce-scatter.31.cloned.1.call-start = ((), (), s32[]{:S(2)}) async-start(), calls=%async_computation.21 | async-start | bytes 2293760 | tf_op jit(solution)/shard_map/reduce_scatter | solution.py:28
  371.6 144.7 %reduce-scatter.29.cloned.1.call-start = ((), (), s32[]{:S(2)}) async-start(), calls=%async_computation.20 | async-start | bytes 2293760 | tf_op jit(solution)/shard_map/reduce_scatter | solution.py:27
  380.3 136.1 %reduce-scatter.33.cloned.1.call-start = ((), (), s32[]{:S(2)}) async-start(), calls=%async_computation.22 | async-start | bytes 2293760 | tf_op jit(solution)/shard_map/reduce_scatter | solution.py:29
  426.1 14.3 %copy-start.11 = (bf16[2,32,2048]{2,1,0:T(8,128)(2,1)S(1)}, bf16[2,32,2048]{2,1,0:T(8,128)(2,1)}, u32[]{:S(2)}) copy-start(bf16[2,32,2048]{2,1,0:T(8,128)(2,1)} %param.7) | copy-start | bytes 786436
  426.1 14.3 %collective-permute-start.1 = (bf16[32,2048]{1,0:T(8,128)(2,1)S(1)}, bf16[32,2048]{1,0:T(8,128)(2,1)S(1)}, u32[]{:S(2)}, u32[]{:S(2)}) collective-permute-start(bf16[32,2048]{1,0:T(8,128)(2,1)S(1)} %get-tuple-element.5), channel_id=1, source_target_pairs={{16,0},{17,1},{18,2},{19,3},{20,4},{21,5},{22,6},{23,7},{24,8},{25... | collective-permute-start | bytes 393224 | tf_op jit(solution)/shard_map/ppermute | solution.py:13
  440.3 25.4 %copy-start.3 = (bf16[128,3584]{1,0:T(8,128)(2,1)S(1)}, bf16[128,3584]{1,0:T(8,128)(2,1)}, u32[]{:S(2)}) copy-start(bf16[128,3584]{1,0:T(8,128)(2,1)} %copy-done.2) | copy-start | bytes 2752516
  453.9 11.5 %copy-start.7 = (bf16[128,2048]{1,0:T(8,128)(2,1)}, bf16[128,2048]{1,0:T(8,128)(2,1)S(1)}, u32[]{:S(2)}) copy-start(bf16[128,2048]{1,0:T(8,128)(2,1)S(1)} %all_gather.54) | copy-start | bytes 1572868
  465.5 12.7 %copy-start.15 = (bf16[32,3584]{1,0:T(8,128)(2,1)S(1)}, bf16[32,3584]{1,0:T(8,128)(2,1)}, u32[]{:S(2)}) copy-start(bf16[32,3584]{1,0:T(8,128)(2,1)} %get-tuple-element.8) | copy-start | bytes 688132
  465.5 27.4 %copy-start.1 = (bf16[128,3584]{1,0:T(8,128)(2,1)S(1)}, bf16[128,3584]{1,0:T(8,128)(2,1)}, u32[]{:S(2)}) copy-start(bf16[128,3584]{1,0:T(8,128)(2,1)} %copy-done) | copy-start | bytes 2752516
  465.5 176.9 %reduce-scatter.35.cloned.1.call-start = ((), (), s32[]{:S(2)}) async-start(), calls=%async_computation.23 | async-start | bytes 1310720 | tf_op jit(solution)/shard_map/reduce_scatter | solution.py:99
  492.9 11.9 %copy-start.6 = (bf16[128,2048]{1,0:T(8,128)(2,1)S(1)}, bf16[128,2048]{1,0:T(8,128)(2,1)}, u32[]{:S(2)}) copy-start(bf16[128,2048]{1,0:T(8,128)(2,1)} %copy-done.5) | copy-start | bytes 1572868
  567.3 25.2 %copy-start.8 = (bf16[128,2048]{1,0:T(8,128)(2,1)S(1)}, bf16[128,2048]{1,0:T(8,128)(2,1)}, u32[]{:S(2)}) copy-start(bf16[128,2048]{1,0:T(8,128)(2,1)} %copy-done.7) | copy-start | bytes 1572868
  617.4 25.0 %copy-start.13 = (bf16[1,2,32,2048]{3,2,1,0:T(8,128)(2,1)S(1)}, bf16[1,2,32,2048]{3,2,1,0:T(8,128)(2,1)}, u32[]{:S(2)}) copy-start(bf16[1,2,32,2048]{3,2,1,0:T(8,128)(2,1)} %get-tuple-element.4) | copy-start | bytes 786436
  (7 other events, 25.1 us)
Sparse Core Ops, SparseCore 0:
  32.1 32.5 reduce-scatter.14
  67.8 29.5 reduce-scatter.12
  99.9 29.5 reduce-scatter.16
  171.7 32.0 reduce-scatter.18
  206.7 28.9 reduce-scatter.22
  238.7 29.5 reduce-scatter.20
  270.8 29.5 reduce-scatter.24
  344.9 32.3 reduce-scatter.26
  380.4 28.8 reduce-scatter.30
  412.3 29.5 reduce-scatter.28
  465.6 34.4 reduce-scatter.32
  557.7 26.1 reduce-scatter.34
where the time goes:
time: 661 us; the launch traced here: 651 us
  matrix products  296 us (45%)
  blocking collectives  184 us (28%)
  waiting for transfers between devices  118 us (18%)
  local copies, waits for them, and re-layouts  22.7 us (3%)
  between operations  14.9 us (2%)
  other arithmetic  10.1 us (2%)
    reduce_scatter x3, waiting for transfers between devices, combine(): lax.psum_scatter(grad_part, 'row', scatter_dimension=0, tiled=True)  64.3 us
    reduce_scatter x3, waiting for transfers between devices, combine(): lax.psum_scatter(gate_part, 'row', scatter_dimension=0, tiled=True)  51.9 us
    all_gather x3, blocking collectives, shards(): lax.all_gather(local_input, 'col', axis=0, tiled=True)  50.5 us
    dot_general x3, matrix products, shards(): jnp.einsum('td,tf->df', rows_input, grad_hgate, preferred_element_type=jn...  49.9 us
    dot_general x3, matrix products, shards(): jnp.einsum('tf,td->fd', hidden, rows_grad, preferred_element_type=jnp.flo...  49.2 us
    dot_general x3, matrix products, shards(): jnp.einsum('td,tf->df', rows_input, grad_up, preferred_element_type=jnp.f...  48.8 us
    all_gather x3, blocking collectives, shards(): lax.all_gather(grad_in, 'col', axis=0, tiled=True)  39.3 us
    all_gather x3, blocking collectives, combine(): lax.all_gather(results[0], 'row', axis=0, tiled=True)  37.1 us
  transfers between devices with their start and end apart: 14, of which 5 were waited for; matrix products, arithmetic and copies ran while one was open for 38% of the time, Pallas kernels for 0%

commit v1 on v0

--- a/solution.py
+++ b/solution.py
@@ -1,3 +1,4 @@
+import functools
 import jax
 import jax.numpy as jnp
 from jax import lax
@@ -5,6 +6,24 @@
 
 BLK = 64
 TB = 64
+
+
+def _take_columns(base_x, axis_key):
+    shares = lax.psum(1, axis_name=axis_key)
+    grid = [base_x]
+    for dev_j in tuple(range(1, shares)):
+        grid.append(
+            lax.ppermute(
+                grid[dev_j - 1],
+                axis_name=axis_key,
+                perm=[(nth, (nth - 1) % shares) for nth in range(shares)],
+            )
+        )
+    x_new = jnp.concatenate(grid, axis=0)
+    return jnp.roll(x_new, lax.axis_index(axis_key) * base_x.shape[0], axis=0)
+
+
+push_layers_all = functools.partial(_take_columns, axis_key="row")
 
 
 def passed_along(value, axis, steps):
@@ -32,7 +51,7 @@
     own_mask = lax.dynamic_slice_in_dim(keep_mask, lax.axis_index("row") * row_count, row_count, 0)
     results = activate(gate_total, up_total, grad_total, own_mask)
     hidden, grad_hgate, grad_up = (
-        lax.all_gather(results[0], "row", axis=0, tiled=True),
+        push_layers_all(results[0]),
         lax.all_gather(results[1], "row", axis=0, tiled=True),
         lax.all_gather(results[2], "row", axis=0, tiled=True),
     )

time: 661 us -> 638 us (0.965)
  blocking collectives: 184 us -> 147 us
  starting transfers between devices: 5.35 us -> 14.5 us
    all_gather x3 -> x0, blocking collectives: 37.1 us -> none  [combine(): lax.all_gather(results[0], 'row', axis=0, tiled=True)]
    ppermute x0 -> x9, starting transfers between devices: none -> 8.98 us  [_take_columns(): lax.ppermute(grid[dev_j - 1], axis_name=axis_key, perm=[(nth, (nth - 1) %...]
  transfers between devices with their start and end apart: 14 -> 23, of which waited for: 5 -> 5; matrix products, arithmetic and copies ran while one was open for 38% -> 43% of each run, Pallas kernels for 0% -> 0%
where the time goes in v1:
time: 638 us; the launch traced here: 628 us
  matrix products  299 us (47%)
  blocking collectives  147 us (23%)
  waiting for transfers between devices  116 us (18%)
  local copies, waits for them, and re-layouts  26 us (4%)
  between operations  14.9 us (2%)
  starting transfers between devices  14.5 us (2%)
  other arithmetic  10.1 us (2%)
    reduce_scatter x3, waiting for transfers between devices, combine(): lax.psum_scatter(grad_part, 'row', scatter_dimension=0, tiled=True)  64.3 us
    dot_general x3, matrix products, shards(): jnp.einsum('tf,td->fd', hidden, rows_grad, preferred_element_type=jnp.flo...  52.4 us
    all_gather x3, blocking collectives, shards(): lax.all_gather(local_input, 'col', axis=0, tiled=True)  51 us
    reduce_scatter x3, waiting for transfers between devices, combine(): lax.psum_scatter(gate_part, 'row', scatter_dimension=0, tiled=True)  49.6 us
    dot_general x3, matrix products, shards(): jnp.einsum('td,tf->df', rows_input, grad_hgate, preferred_element_type=jn...  49.5 us
    dot_general x3, matrix products, shards(): jnp.einsum('td,tf->df', rows_input, grad_up, preferred_element_type=jnp.f...  48.5 us
    all_gather x3, blocking collectives, shards(): lax.all_gather(grad_in, 'col', axis=0, tiled=True)  39.3 us
    dot_general x3, matrix products, shards(): jnp.einsum('td,fd->tf', rows_grad, w_down, preferred_element_type=jnp.flo...  34.4 us
  transfers between devices with their start and end apart: 23, of which 5 were waited for; matrix products, arithmetic and copies ran while one was open for 43% of the time, Pallas kernels for 0%

profile of v1, /device:TPU:3, one launch (start us, length us, event | category | flops | bytes accessed | tf_op | source)
XLA Modules:
  0.0 627.8 jit_solution(4371396703627289142)
XLA Ops:
  8.9 14.5 %all-gather = bf16[1,1,128,2048]{3,2,1,0:T(8,128)(2,1)S(1)} all-gather(bf16[1,1,32,2048]{3,2,1,0:T(8,128)(2,1)S(1)} %get-tuple-element.19), channel_id=2, replica_groups=mesh['section'=2,'row'=4,'col'=4] {'col'}, dimensions={2}, use_global_device_ids=true | all-gather | bytes 655360 | tf_op jit(solution)/shard_map/all_gather | solution.py:85
  41.5 11.9 %all-gather.1 = bf16[1,128,2048]{2,1,0:T(8,128)(2,1)S(1)} all-gather(bf16[1,32,2048]{2,1,0:T(8,128)(2,1)S(1)} %dynamic-slice_select_fusion), channel_id=3, replica_groups=mesh['section'=2,'row'=4,'col'=4] {'col'}, dimensions={1}, use_global_device_ids=true | all-gather | bytes 655360 | tf_op jit(solution)/shard_map/all_gather | solution.py:86
  54.2 11.4 %fusion.4 = f32[128,3584]{1,0:T(8,128)} fusion(bf16[1,3584,2048]{2,1,0:T(8,128)(2,1)} %param.12, bf16[1,128,2048]{2,1,0:T(8,128)(2,1)S(1)} %all-gather.1), kind=kOutput, calls=%fused_computation.7 | convolution fusion | flops 1879048192 | bytes 17039360 | tf_op jit(solution)/shard_map/td,fd->tf/dot_general | solution.py:101
  71.6 25.8 %reduce-scatter.13.cloned.1.call-done = f32[32,3584]{1,0:T(8,128)} async-done(((f32[128,3584]{1,0:T(8,128)}), f32[32,3584]{1,0:T(8,128)}) %reduce-scatter.13.cloned.1.call-update) | async-done | bytes 458768 | tf_op jit(solution)/shard_map/reduce_scatter | solution.py:46
  97.4 32.2 %reduce-scatter.17.cloned.1.call-done = f32[32,3584]{1,0:T(8,128)} async-done(((f32[128,3584]{1,0:T(8,128)}), f32[32,3584]{1,0:T(8,128)}) %reduce-scatter.17.cloned.1.call-update) | async-done | bytes 458768 | tf_op jit(solution)/shard_map/reduce_scatter | solution.py:48
  171.6 17.7 %all-gather.2 = bf16[1,1,128,2048]{3,2,1,0:T(8,128)(2,1)S(1)} all-gather(bf16[1,1,32,2048]{3,2,1,0:T(8,128)(2,1)S(1)} %get-tuple-element.20), channel_id=4, replica_groups=mesh['section'=2,'row'=4,'col'=4] {'col'}, dimensions={2}, use_global_device_ids=true | all-gather | bytes 655360 | tf_op jit(solution)/shard_map/all_gather | solution.py:85
  213.2 13.4 %all_gather.41 = bf16[128,2048]{1,0:T(8,128)(2,1)S(1)} all-gather(bf16[32,2048]{1,0:T(8,128)(2,1)S(1)} %bitcast_select_fusion.2), channel_id=1, replica_groups=mesh['section'=2,'row'=4,'col'=4] {'col'}, dimensions={0}, use_global_device_ids=true | all-gather | bytes 655360 | tf_op jit(solution)/shard_map/all_gather | solution.py:86
  226.6 11.6 %fusion.2 = f32[128,3584]{1,0:T(8,128)} fusion(bf16[128,2048]{1,0:T(8,128)(2,1)S(1)} %all_gather.41, bf16[1,3584,2048]{2,1,0:T(8,128)(2,1)} %param.12), kind=kOutput, calls=%fused_computation.5 | convolution fusion | flops 1879048192 | bytes 17039360 | tf_op jit(solution)/shard_map/td,fd->tf/dot_general | solution.py:101
  244.6 23.7 %reduce-scatter.21.cloned.1.call-done = f32[32,3584]{1,0:T(8,128)} async-done(((f32[128,3584]{1,0:T(8,128)}), f32[32,3584]{1,0:T(8,128)}) %reduce-scatter.21.cloned.1.call-update) | async-done | bytes 458768 | tf_op jit(solution)/shard_map/reduce_scatter | solution.py:46
  268.3 32.2 %reduce-scatter.25.cloned.1.call-done = f32[32,3584]{1,0:T(8,128)} async-done(((f32[128,3584]{1,0:T(8,128)}), f32[32,3584]{1,0:T(8,128)}) %reduce-scatter.25.cloned.1.call-update) | async-done | bytes 458768 | tf_op jit(solution)/shard_map/reduce_scatter | solution.py:48
  333.2 11.0 %fusion.36 = f32[128,2048]{1,0:T(8,128)} fusion(f32[128,2048]{1,0:T(8,128)S(1)} %fusion.10, bf16[128,3584]{1,0:T(8,128)(2,1)S(1)} %all_gather.42, bf16[1,2048,3584]{2,1,0:T(8,128)(2,1)} %param.10), kind=kOutput, calls=%fused_computation.37 | convolution fusion | flops 1879310336 | bytes 17694720 | tf_op jit(solution)/shard_map/tf,df->td/dot_general | solution.py:112
  344.3 18.8 %all-gather.3 = bf16[1,1,128,2048]{3,2,1,0:T(8,128)(2,1)S(1)} all-gather(bf16[1,1,32,2048]{3,2,1,0:T(8,128)(2,1)} %get-tuple-element.18), channel_id=5, replica_groups=mesh['section'=2,'row'=4,'col'=4] {'col'}, dimensions={2}, use_global_device_ids=true | all-gather | bytes 655360 | tf_op jit(solution)/shard_map/all_gather | solution.py:85
  389.8 12.0 %fusion.85 = f32[2048,3584]{1,0:T(8,128)} fusion(bf16[128,3584]{1,0:T(8,128)(2,1)S(1)} %all_gather.38, bf16[1,1,128,2048]{3,2,1,0:T(8,128)(2,1)S(1)} %all-gather), kind=kOutput, calls=%fused_computation.103 | convolution fusion | flops 1879048192 | bytes 30801920 | tf_op jit(solution)/shard_map/td,tf->df/dot_general | solution.py:103
  406.9 11.8 %fusion.83 = f32[2048,3584]{1,0:T(8,128)} fusion(bf16[128,3584]{1,0:T(8,128)(2,1)S(1)} %all_gather.39, bf16[1,1,128,2048]{3,2,1,0:T(8,128)(2,1)S(1)} %all-gather), kind=kOutput, calls=%fused_computation.101 | convolution fusion | flops 1879048192 | bytes 30801920 | tf_op jit(solution)/shard_map/td,tf->df/dot_general | solution.py:106
  420.0 14.0 %all_gather.45 = bf16[128,2048]{1,0:T(8,128)(2,1)S(1)} all-gather(bf16[32,2048]{1,0:T(8,128)(2,1)S(1)} %bitcast_select_fusion), channel_id=1, replica_groups=mesh['section'=2,'row'=4,'col'=4] {'col'}, dimensions={0}, use_global_device_ids=true | all-gather | bytes 655360 | tf_op jit(solution)/shard_map/all_gather | solution.py:86
  434.8 11.4 %fusion = f32[128,3584]{1,0:T(8,128)} fusion(bf16[128,2048]{1,0:T(8,128)(2,1)S(1)} %all_gather.45, bf16[1,3584,2048]{2,1,0:T(8,128)(2,1)} %param.12), kind=kOutput, calls=%fused_computation.3 | convolution fusion | flops 1879048192 | bytes 17039360 | tf_op jit(solution)/shard_map/td,fd->tf/dot_general | solution.py:101
  447.4 12.3 %fusion.77 = f32[2048,3584]{1,0:T(8,128)} fusion(bf16[128,3584]{1,0:T(8,128)(2,1)S(1)} %copy-done.3, bf16[1,1,128,2048]{3,2,1,0:T(8,128)(2,1)S(1)} %all-gather.2), kind=kOutput, calls=%fused_computation.95 | convolution fusion | flops 1879048192 | bytes 30801920 | tf_op jit(solution)/shard_map/td,tf->df/dot_general | solution.py:103
  461.7 11.8 %fusion.75 = f32[2048,3584]{1,0:T(8,128)} fusion(bf16[128,3584]{1,0:T(8,128)(2,1)S(1)} %copy-done.1, bf16[1,1,128,2048]{3,2,1,0:T(8,128)(2,1)S(1)} %all-gather.2), kind=kOutput, calls=%fused_computation.93 | convolution fusion | flops 1879048192 | bytes 30801920 | tf_op jit(solution)/shard_map/td,tf->df/dot_general | solution.py:106
  473.5 13.8 %fusion.56 = f32[3584,2048]{1,0:T(8,128)} fusion(bf16[128,2048]{1,0:T(8,128)(2,1)S(1)} %copy-done.7, s32[]{:T(128)S(6)} %select_n.106, bf16[32,3584]{1,0:T(8,128)(2,1)} %get-tuple-element.12, bf16[32,3584]{1,0:T(8,128)(2,1)} %collective-permute-done.5, bf16[32,3584]{1,0:T(8,128)(2,1)S(1)} %collective-permute-done.6, ...), kind=kOutput, calls=%fused_computation.75 | convolution fusion | flops 1886388224 | bytes 30801924 | tf_op jit(solution)/shard_map/tf,td->fd/dot_general | solution.py:109
  517.8 11.0 %fusion.39 = f32[128,2048]{1,0:T(8,128)} fusion(f32[128,2048]{1,0:T(8,128)S(1)} %fusion.6, bf16[128,3584]{1,0:T(8,128)(2,1)S(1)} %all_gather.46, bf16[1,2048,3584]{2,1,0:T(8,128)(2,1)} %param.10), kind=kOutput, calls=%fused_computation.38 | convolution fusion | flops 1879310336 | bytes 17694720 | tf_op jit(solution)/shard_map/tf,df->td/dot_general | solution.py:112
  529.7 25.1 %fusion.30 = bf16[1,2048,3584]{2,1,0:T(8,128)(2,1)} fusion(bf16[128,3584]{1,0:T(8,128)(2,1)S(1)} %all_gather.46, f32[2048,3584]{1,0:T(8,128)} %fusion.85, f32[2048,3584]{1,0:T(8,128)} %fusion.77, bf16[1,1,128,2048]{3,2,1,0:T(8,128)(2,1)S(1)} %all-gather.3), kind=kOutput, calls=%fused_computation.33 | convolution fusion | flops 1901068288 | bytes 74842112 | tf_op jit(solution)/shard_map/td,tf->df/dot_general | solution.py:103
  555.2 25.0 %fusion.31 = bf16[1,2048,3584]{2,1,0:T(8,128)(2,1)} fusion(bf16[128,3584]{1,0:T(8,128)(2,1)S(1)} %all_gather.47, f32[2048,3584]{1,0:T(8,128)} %fusion.83, f32[2048,3584]{1,0:T(8,128)} %fusion.75, bf16[1,1,128,2048]{3,2,1,0:T(8,128)(2,1)S(1)} %all-gather.3), kind=kOutput, calls=%fused_computation.34 | convolution fusion | flops 1901068288 | bytes 74842112 | tf_op jit(solution)/shard_map/td,tf->df/dot_general | solution.py:106
  580.2 12.5 %fusion.46 = f32[3584,2048]{1,0:T(8,128)} fusion(bf16[128,2048]{1,0:T(8,128)(2,1)S(1)} %copy-done.9, s32[]{:T(128)S(6)} %select_n.106, bf16[32,3584]{1,0:T(8,128)(2,1)S(1)} %get-tuple-element.15, bf16[32,3584]{1,0:T(8,128)(2,1)S(1)} %collective-permute-done.8, bf16[32,3584]{1,0:T(8,128)(2,1)S(1)} %collective-permute-done.9, ...), kind=kOutput, calls=%fused_computation.67 | convolution fusion | flops 1886388224 | bytes 30801924 | tf_op jit(solution)/shard_map/tf,td->fd/dot_general | solution.py:109
  592.7 26.1 %fusion.32 = bf16[1,3584,2048]{2,1,0:T(8,128)(2,1)} fusion(f32[3584,2048]{1,0:T(8,128)} %fusion.46, f32[3584,2048]{1,0:T(8,128)} %fusion.56, s32[]{:T(128)S(6)} %select_n.106, bf16[32,3584]{1,0:T(8,128)(2,1)S(1)} %copy-done.16, bf16[32,3584]{1,0:T(8,128)(2,1)} %collective-permute-done.2, bf16[32,3584]{1,0:T(8,128)(2,1)} %collective-permute-done.3, ...), kind=kOutput, calls=%fused_computation.35 | convolution fusion | flops 1908408320 | bytes 74842112 | tf_op jit(solution)/shard_map/tf,td->fd/dot_general | solution.py:109
  (130 shorter events, 202.1 us)
Async XLA Ops:
  7.2 64.4 %reduce-scatter.15.cloned.1.call-start = ((), (), s32[]{:S(2)}) async-start(), calls=%async_computation.13 | async-start | bytes 2293760 | tf_op jit(solution)/shard_map/reduce_scatter | solution.py:47
  31.9 65.4 %reduce-scatter.13.cloned.1.call-start = ((), (), s32[]{:S(2)}) async-start(), calls=%async_computation.12 | async-start | bytes 2293760 | tf_op jit(solution)/shard_map/reduce_scatter | solution.py:46
  40.5 89.1 %reduce-scatter.17.cloned.1.call-start = ((), (), s32[]{:S(2)}) async-start(), calls=%async_computation.14 | async-start | bytes 2293760 | tf_op jit(solution)/shard_map/reduce_scatter | solution.py:48
  65.6 141.0 %reduce-scatter.19.cloned.1.call-start = ((), (), s32[]{:S(2)}) async-start(), calls=%async_computation.15 | async-start | bytes 1310720 | tf_op jit(solution)/shard_map/reduce_scatter | solution.py:118
  171.6 73.0 %reduce-scatter.23.cloned.1.call-start = ((), (), s32[]{:S(2)}) async-start(), calls=%async_computation.17 | async-start | bytes 2293760 | tf_op jit(solution)/shard_map/reduce_scatter | solution.py:47
  197.9 70.4 %reduce-scatter.21.cloned.1.call-start = ((), (), s32[]{:S(2)}) async-start(), calls=%async_computation.16 | async-start | bytes 2293760 | tf_op jit(solution)/shard_map/reduce_scatter | solution.py:46
  206.6 93.9 %reduce-scatter.25.cloned.1.call-start = ((), (), s32[]{:S(2)}) async-start(), calls=%async_computation.18 | async-start | bytes 2293760 | tf_op jit(solution)/shard_map/reduce_scatter | solution.py:48
  208.5 4.6 collective-permute-start
  238.2 164.7 %reduce-scatter.27.cloned.1.call-start = ((), (), s32[]{:S(2)}) async-start(), calls=%async_computation.19 | async-start | bytes 1310720 | tf_op jit(solution)/shard_map/reduce_scatter | solution.py:118
  344.2 143.1 %reduce-scatter.31.cloned.1.call-start = ((), (), s32[]{:S(2)}) async-start(), calls=%async_computation.21 | async-start | bytes 2293760 | tf_op jit(solution)/shard_map/reduce_scatter | solution.py:47
  371.6 115.7 %reduce-scatter.29.cloned.1.call-start = ((), (), s32[]{:S(2)}) async-start(), calls=%async_computation.20 | async-start | bytes 2293760 | tf_op jit(solution)/shard_map/reduce_scatter | solution.py:46
  380.2 107.0 %reduce-scatter.33.cloned.1.call-start = ((), (), s32[]{:S(2)}) async-start(), calls=%async_computation.22 | async-start | bytes 2293760 | tf_op jit(solution)/shard_map/reduce_scatter | solution.py:48
  386.6 15.1 %collective-permute-start.2 = (bf16[32,3584]{1,0:T(8,128)(2,1)}, bf16[32,3584]{1,0:T(8,128)(2,1)}, u32[]{:S(2)}, u32[]{:S(2)}) collective-permute-start(bf16[32,3584]{1,0:T(8,128)(2,1)} %get-tuple-element.9), channel_id=1, source_target_pairs={{0,12},{4,0},{8,4},{12,8},{1,13},{5,1},{9,5},{13,9},{2,14},{6,2},{... | collective-permute-start | bytes 688136 | tf_op jit(solution)/shard_map/ppermute | solution.py:16
  401.7 17.0 %collective-permute-start.3 = (bf16[32,3584]{1,0:T(8,128)(2,1)}, bf16[32,3584]{1,0:T(8,128)(2,1)}, u32[]{:S(2)}, u32[]{:S(2)}) collective-permute-start(bf16[32,3584]{1,0:T(8,128)(2,1)} %collective-permute-done.2), channel_id=1, source_target_pairs={{0,12},{4,0},{8,4},{12,8},{1,13},{5,1},{9,5},{13,9},{2,14},{6,2},{... | collective-permute-start | bytes 688136 | tf_op jit(solution)/shard_map/ppermute | solution.py:16
  401.7 17.3 %collective-permute-start.5 = (bf16[32,3584]{1,0:T(8,128)(2,1)}, bf16[32,3584]{1,0:T(8,128)(2,1)}, u32[]{:S(2)}, u32[]{:S(2)}) collective-permute-start(bf16[32,3584]{1,0:T(8,128)(2,1)} %get-tuple-element.12), channel_id=1, source_target_pairs={{0,12},{4,0},{8,4},{12,8},{1,13},{5,1},{9,5},{13,9},{2,14},{6,2},{... | collective-permute-start | bytes 688136 | tf_op jit(solution)/shard_map/ppermute | solution.py:16
  404.6 15.4 %collective-permute-start.1 = (bf16[32,2048]{1,0:T(8,128)(2,1)S(1)}, bf16[32,2048]{1,0:T(8,128)(2,1)S(1)}, u32[]{:S(2)}, u32[]{:S(2)}) collective-permute-start(bf16[32,2048]{1,0:T(8,128)(2,1)S(1)} %get-tuple-element.6), channel_id=1, source_target_pairs={{16,0},{17,1},{18,2},{19,3},{20,4},{21,5},{22,6},{23,7},{24,8},{25... | collective-permute-start | bytes 393224 | tf_op jit(solution)/shard_map/ppermute | solution.py:32
  418.7 174.0 %collective-permute-start.4 = (bf16[32,3584]{1,0:T(8,128)(2,1)}, bf16[32,3584]{1,0:T(8,128)(2,1)}, u32[]{:S(2)}, u32[]{:S(2)}) collective-permute-start(bf16[32,3584]{1,0:T(8,128)(2,1)} %collective-permute-done.3), channel_id=1, source_target_pairs={{0,12},{4,0},{8,4},{12,8},{1,13},{5,1},{9,5},{13,9},{2,14},{6,2},{... | collective-permute-start | bytes 688136 | tf_op jit(solution)/shard_map/ppermute | solution.py:16
  419.0 40.7 %collective-permute-start.6 = (bf16[32,3584]{1,0:T(8,128)(2,1)}, bf16[32,3584]{1,0:T(8,128)(2,1)S(1)}, u32[]{:S(2)}, u32[]{:S(2)}) collective-permute-start(bf16[32,3584]{1,0:T(8,128)(2,1)} %collective-permute-done.5), channel_id=1, source_target_pairs={{0,12},{4,0},{8,4},{12,8},{1,13},{5,1},{9,5},{13,9},{2,14},{6,2},{... | collective-permute-start | bytes 688136 | tf_op jit(solution)/shard_map/ppermute | solution.py:16
  446.2 172.6 %reduce-scatter.35.cloned.1.call-start = ((), (), s32[]{:S(2)}) async-start(), calls=%async_computation.23 | async-start | bytes 1310720 | tf_op jit(solution)/shard_map/reduce_scatter | solution.py:118
  459.7 13.7 %collective-permute-start.7 = (bf16[32,3584]{1,0:T(8,128)(2,1)S(1)}, bf16[32,3584]{1,0:T(8,128)(2,1)S(1)}, u32[]{:S(2)}, u32[]{:S(2)}) collective-permute-start(bf16[32,3584]{1,0:T(8,128)(2,1)S(1)} %collective-permute-done.6), channel_id=1, source_target_pairs={{0,12},{4,0},{8,4},{12,8},{1,13},{5,1},{9,5},{13,9},{2,14},{6,2},{... | collective-permute-start | bytes 688136 | tf_op jit(solution)/shard_map/ppermute | solution.py:16
  517.6 11.1 %collective-permute-start.8 = (bf16[32,3584]{1,0:T(8,128)(2,1)S(1)}, bf16[32,3584]{1,0:T(8,128)(2,1)S(1)}, u32[]{:S(2)}, u32[]{:S(2)}) collective-permute-start(bf16[32,3584]{1,0:T(8,128)(2,1)S(1)} %get-tuple-element.15), channel_id=1, source_target_pairs={{0,12},{4,0},{8,4},{12,8},{1,13},{5,1},{9,5},{13,9},{2,14},{6,2},{... | collective-permute-start | bytes 688136 | tf_op jit(solution)/shard_map/ppermute | solution.py:16
  528.8 26.1 %collective-permute-start.9 = (bf16[32,3584]{1,0:T(8,128)(2,1)S(1)}, bf16[32,3584]{1,0:T(8,128)(2,1)S(1)}, u32[]{:S(2)}, u32[]{:S(2)}) collective-permute-start(bf16[32,3584]{1,0:T(8,128)(2,1)S(1)} %collective-permute-done.8), channel_id=1, source_target_pairs={{0,12},{4,0},{8,4},{12,8},{1,13},{5,1},{9,5},{13,9},{2,14},{6,2},{... | collective-permute-start | bytes 688136 | tf_op jit(solution)/shard_map/ppermute | solution.py:16
  554.8 25.4 %collective-permute-start.10 = (bf16[32,3584]{1,0:T(8,128)(2,1)S(1)}, bf16[32,3584]{1,0:T(8,128)(2,1)S(1)}, u32[]{:S(2)}, u32[]{:S(2)}) collective-permute-start(bf16[32,3584]{1,0:T(8,128)(2,1)S(1)} %collective-permute-done.9), channel_id=1, source_target_pairs={{0,12},{4,0},{8,4},{12,8},{1,13},{5,1},{9,5},{13,9},{2,14},{6,2},{... | collective-permute-start | bytes 688136 | tf_op jit(solution)/shard_map/ppermute | solution.py:16
  592.7 26.1 %copy-start.14 = (bf16[1,2,32,2048]{3,2,1,0:T(8,128)(2,1)S(1)}, bf16[1,2,32,2048]{3,2,1,0:T(8,128)(2,1)}, u32[]{:S(2)}) copy-start(bf16[1,2,32,2048]{3,2,1,0:T(8,128)(2,1)} %get-tuple-element.5) | copy-start | bytes 786436
  (17 other events, 128.5 us)
Sparse Core Ops, SparseCore 0:
  32.1 32.5 reduce-scatter.14
  67.8 29.5 reduce-scatter.12
  99.9 29.5 reduce-scatter.16
  171.7 31.9 reduce-scatter.18
  206.6 29.0 reduce-scatter.22
  238.7 29.5 reduce-scatter.20
  270.8 29.5 reduce-scatter.24
  344.3 32.3 reduce-scatter.26
  379.9 29.9 reduce-scatter.30
  412.8 30.1 reduce-scatter.28
  446.4 30.9 reduce-scatter.32
  528.9 28.1 reduce-scatter.34
